TPU v7x, 32 devices: a whole 2x2x4 slice. The times are simulated.
32 devices in a mesh: req: 4 (over z), exp: 8 (over y, x, core).
Axes of the slice: x: 2, y: 2, z: 4, core: 2. Of those that a mesh axis runs over, the one named last changes fastest.
Arguments:
- queries: bfloat16 [64, 32, 2304], P(('req', 'exp')), may hold values from -8 to 8
- draft_keys: bfloat16 [64, 32, 2304], P(('req', 'exp')), may hold values from -9 to 9
- draft_values: bfloat16 [64, 32, 2304], P(('req', 'exp')), may hold values from -6 to 6
- tree_parents: int32 [64, 32], P(('req', 'exp')), may hold values from -1 to 30, as said below
- cache_keys: bfloat16 [64, 768, 2304], P(('req', 'exp')), may hold values from -9 to 9
- cache_values: bfloat16 [64, 768, 2304], P(('req', 'exp')), may hold values from -6 to 6
- cache_lengths: int32 [64], P(('req', 'exp')), may hold values from 1 to 768, as said below
- prompt_keys: bfloat16 [8, 512, 2304], P('req', 'exp'), may hold values from -9 to 9
- prompt_values: bfloat16 [8, 512, 2304], P('req', 'exp'), may hold values from -6 to 6
- group_ids: int32 [64], P(('req', 'exp')), may hold values from 0 to 1
- residual: bfloat16 [64, 32, 2304], P(('req', 'exp')), may hold values from -6 to 6
- norm_gain: float32 [2304], replicated, may hold values from 0.5 to 1.5
- router: bfloat16 [2304, 8], replicated, may hold values from -0.125 to 0.125
- w_gate: bfloat16 [8, 2304, 5760], P('exp', None, 'req'), may hold values from -0.125 to 0.125
- w_up: bfloat16 [8, 2304, 5760], P('exp', None, 'req'), may hold values from -0.125 to 0.125
- w_down: bfloat16 [8, 5760, 2304], P('exp', 'req'), may hold values from -0.078125 to 0.078125
- expert_ids: int32 [64, 32, 2], P(('req', 'exp')), may hold values from 0 to 7, all different within a row; in each aligned block of 64 rows (0 to 63, 64 to 127, ..., all dimensions but the last counted through in order) at most 18 rows name the same one
- accepted_rows: int32 [64, 8], P(('req', 'exp')), may hold values from 0 to 31
Outputs:
- attended: bfloat16 [64, 32, 2304], P(('req', 'exp'))
- layer_out: bfloat16 [64, 32, 2304], P(('req', 'exp'))
- accepted_cache: bfloat16 [64, 2, 8, 2304], P(('req', 'exp'))
Inputs may be any that keep to these rules, and one draw needn't show every extreme that they name: `tree_parents`: position 0 of every tree holds -1; every other position holds an earlier position of the same tree. `cache_lengths`: some request has all 768 slots used. `expert_ids`: the two experts of a position differ; among the rows of one device no expert is named more than 18 times, a bound that some block reaches.
All inputs are finite; a program needn't handle non-finite values.
Results may differ from a plain program's by a relative error of at most 0.013.
Values may be sent and summed in bfloat16 or wider, within the bound.
A program may use at most 192 MiB of HBM per device.

v0:
```python
import jax
import jax.numpy as jnp
from jax import lax
from jax.sharding import PartitionSpec as P

HEADS = 36
HDIM = 64
EXPERTS = 8
TOPK = 2
GRP = 2
CAP = 18
HIGH = lax.Precision.HIGHEST
EPSILON = 1e-05


def ancestry(parents):
    length = parents.shape[-1]
    column = jnp.arange(length, dtype=jnp.int32)
    reached = (parents[..., :, None] == column).astype(jnp.float32) + jnp.eye(
        length, dtype=jnp.float32
    )
    for repeat in range(max(1, (length - 1).bit_length())):
        reached = (jnp.einsum("...ij,...jk->...ik", reached, reached, precision=HIGH) > 0.5).astype(
            jnp.float32
        )
    return reached > 0.5


def slot_numbers(picked_ids):
    flattened = picked_ids.reshape(-1)
    onehot = (flattened[:, None] == jnp.arange(EXPERTS, dtype=jnp.int32)[None, :]).astype(jnp.int32)
    before = jnp.cumsum(onehot, axis=0) - onehot
    return jnp.sum(before * onehot, axis=1).reshape(picked_ids.shape)


def on_device(
    queries,
    draft_keys,
    draft_values,
    tree_parents,
    cache_keys,
    cache_values,
    cache_lengths,
    prompt_keys,
    prompt_values,
    group_ids,
    residual,
    norm_gain,
    router,
    w_gate,
    w_up,
    w_down,
    expert_ids,
    accepted_rows,
):
    requests, tree_len, width = queries.shape
    row_count = requests * tree_len
    score_scale = HDIM ** (-0.5)
    heads_q = queries.reshape(requests, tree_len, HEADS, HDIM)
    cache_heads = cache_keys.reshape(requests, -1, HEADS, HDIM)
    cache_vals = cache_values.reshape(requests, -1, HEADS, HDIM)
    cache_scores = (
        jnp.einsum("bthd,bchd->bthc", heads_q, cache_heads, preferred_element_type=jnp.float32)
        * score_scale
    )
    live_cache = jnp.arange(cache_heads.shape[1], dtype=jnp.int32)[None, :] < cache_lengths[:, None]
    cache_scores = jnp.where(live_cache[:, None, None, :], cache_scores, -jnp.inf)
    draft_heads = draft_keys.reshape(requests, tree_len, HEADS, HDIM)
    draft_vals = draft_values.reshape(requests, tree_len, HEADS, HDIM)
    tree_scores = (
        jnp.einsum("bthd,bshd->bths", heads_q, draft_heads, preferred_element_type=jnp.float32)
        * score_scale
    )
    tree_scores = jnp.where(ancestry(tree_parents)[:, :, None, :], tree_scores, -jnp.inf)
    local_top = jnp.maximum(jnp.max(cache_scores, axis=-1), jnp.max(tree_scores, axis=-1))
    cache_weights = jnp.exp(cache_scores - local_top[..., None])
    tree_weights = jnp.exp(tree_scores - local_top[..., None])
    local_total = jnp.sum(cache_weights, axis=-1) + jnp.sum(tree_weights, axis=-1)
    local_acc = jnp.einsum(
        "bthc,bchd->bthd",
        cache_weights.astype(jnp.bfloat16),
        cache_vals,
        preferred_element_type=jnp.float32,
    )
    local_acc = local_acc + jnp.einsum(
        "bths,bshd->bthd",
        tree_weights.astype(jnp.bfloat16),
        draft_vals,
        preferred_element_type=jnp.float32,
    )
    local_top = local_top.reshape(row_count, HEADS)
    local_total = local_total.reshape(row_count, HEADS)
    local_acc = local_acc.reshape(row_count, HEADS, HDIM)
    member = jnp.repeat(group_ids, tree_len)[:, None] == jnp.arange(GRP, dtype=jnp.int32)[None, :]
    query_rows = heads_q.reshape(row_count, HEADS, HDIM)
    running_top = local_top
    summed = local_total
    gathered_acc = local_acc
    key_piece = lax.all_gather(prompt_keys, "exp", axis=1, tiled=True)
    value_piece = lax.all_gather(prompt_values, "exp", axis=1, tiled=True)
    key_count = key_piece.shape[1]
    key_heads = key_piece.reshape(GRP, key_count, HEADS, HDIM)
    value_heads = value_piece.reshape(GRP, key_count, HEADS, HDIM)
    block_scores = (
        jnp.einsum("rhd,gkhd->rhgk", query_rows, key_heads, preferred_element_type=jnp.float32)
        * score_scale
    )
    block_scores = jnp.where(member[:, None, :, None], block_scores, -jnp.inf)
    new_top = jnp.maximum(running_top, jnp.max(block_scores, axis=(2, 3)))
    shrink = jnp.exp(running_top - new_top)
    block_weights = jnp.exp(block_scores - new_top[:, :, None, None])
    summed = summed * shrink + jnp.sum(block_weights, axis=(2, 3))
    gathered_acc = gathered_acc * shrink[:, :, None] + jnp.einsum(
        "rhgk,gkhd->rhd",
        block_weights.astype(jnp.bfloat16),
        value_heads,
        preferred_element_type=jnp.float32,
    )
    running_top, summed, gathered_acc = (new_top, summed, gathered_acc)
    attended = (
        (gathered_acc / summed[:, :, None]).reshape(requests, tree_len, width).astype(jnp.bfloat16)
    )
    stream = (residual.astype(jnp.float32) + attended.astype(jnp.float32)).astype(jnp.bfloat16)
    stream_rows = stream.reshape(row_count, width).astype(jnp.float32)
    normed = (
        stream_rows
        * lax.rsqrt(jnp.mean(stream_rows * stream_rows, axis=-1, keepdims=True) + EPSILON)
        * norm_gain
    ).astype(jnp.bfloat16)
    logits = jnp.dot(normed, router, preferred_element_type=jnp.float32)
    routed = expert_ids.reshape(row_count, TOPK)
    chosen = jnp.take_along_axis(logits, routed, axis=1)
    gate_first = 1.0 / (1.0 + jnp.exp(chosen[:, 1] - chosen[:, 0]))
    gates = jnp.stack([gate_first, 1.0 - gate_first], axis=1)
    target = routed * CAP + slot_numbers(routed)
    buffer = (
        jnp.zeros((EXPERTS * CAP, width), jnp.bfloat16)
        .at[target.reshape(-1)]
        .set(jnp.repeat(normed, TOPK, axis=0))
    )
    holder_count = lax.axis_size("exp")
    holders = holder_count // EXPERTS
    outgoing = jnp.broadcast_to(
        buffer.reshape(EXPERTS, 1, CAP, width), (EXPERTS, holders, CAP, width)
    ).reshape(holder_count, CAP, width)
    gate_local = w_gate[0]
    up_local = w_up[0]
    down_local = w_down[0]
    arrived = lax.all_to_all(outgoing, "exp", split_axis=0, concat_axis=0, tiled=True)
    row_piece = lax.all_gather(arrived.reshape(-1, width), "req", axis=0, tiled=True)
    gate_proj = jnp.dot(row_piece, gate_local, preferred_element_type=jnp.float32)
    up_proj = jnp.dot(row_piece, up_local, preferred_element_type=jnp.float32)
    hidden = (jax.nn.silu(gate_proj) * up_proj).astype(jnp.bfloat16)
    summed_rows = lax.psum_scatter(
        jnp.dot(hidden, down_local, preferred_element_type=jnp.float32).astype(jnp.bfloat16),
        "req",
        scatter_dimension=0,
        tiled=True,
    )
    returned = lax.all_to_all(
        summed_rows.reshape(holder_count, CAP, width),
        "exp",
        split_axis=0,
        concat_axis=0,
        tiled=True,
    )
    expert_result = (
        returned.astype(jnp.float32)
        .reshape(EXPERTS, holders, CAP, width)
        .sum(axis=1)
        .reshape(EXPERTS * CAP, width)
    )
    picked = expert_result[target]
    layer_out = (
        (stream_rows + jnp.sum(gates[:, :, None] * picked, axis=1))
        .astype(jnp.bfloat16)
        .reshape(requests, tree_len, width)
    )
    kept_keys = jnp.take_along_axis(draft_keys, accepted_rows[:, :, None], axis=1)
    kept_values = jnp.take_along_axis(draft_values, accepted_rows[:, :, None], axis=1)
    accepted_cache = jnp.stack([kept_keys, kept_values], axis=1)
    return (attended, layer_out, accepted_cache)


def solution(mesh):
    return jax.shard_map(
        on_device,
        mesh=mesh,
        in_specs=(
            P(("req", "exp"), None, None),
            P(("req", "exp"), None, None),
            P(("req", "exp"), None, None),
            P(("req", "exp"), None),
            P(("req", "exp"), None, None),
            P(("req", "exp"), None, None),
            P(("req", "exp")),
            P("req", "exp", None),
            P("req", "exp", None),
            P(("req", "exp")),
            P(("req", "exp"), None, None),
            P(),
            P(),
            P("exp", None, "req"),
            P("exp", None, "req"),
            P("exp", "req", None),
            P(("req", "exp"), None, None),
            P(("req", "exp"), None),
        ),
        out_specs=(
            P(("req", "exp"), None, None),
            P(("req", "exp"), None, None),
            P(("req", "exp"), None, None, None),
        ),
        check_vma=False,
    )
```

profile of v0, /device:TPU:0, one launch (start us, length us, event | category | flops | bytes accessed | tf_op | source)
XLA Modules:
  0.0 296.1 jit_solution(12981081108997633056)
XLA Ops:
  7.2 2.5 copy.75
  9.8 2.5 copy.79
  12.4 1.4 reshape.291
  13.8 2.5 reshape_reshape.6
  16.4 10.3 %copy.70 = bf16[2,768,2304]{1,2,0:T(8,128)(2,1)} copy(bf16[2,768,2304]{2,1,0:T(8,128)(2,1)} %param.25) | data formatting | bytes 14155776 | tf_op args[5]
  26.7 10.4 %copy.65 = bf16[2,768,2304]{1,2,0:T(8,128)(2,1)} copy(bf16[2,768,2304]{2,1,0:T(8,128)(2,1)} %param.24) | data formatting | bytes 14155776 | tf_op args[4]
  37.1 0.5 reshape.292
  37.6 0.2 fusion.59
  38.6 1.4 reshape.294
  40.0 1.4 fusion.107
  41.4 4.9 %bitcast_reduce_fusion = (f32[2,32,36]{1,2,0:T(8,128)S(1)}, f32[2,36,768,32]{2,3,1,0:T(8,128)S(1)}) fusion(pred[2,768]{1,0:T(4,128)(4,1)S(1)} %iota_compare_fusion.4, bf16[2,768,36,64]{1,3,2,0:T(8,128)(2,1)} %bitcast.124, bf16[2,32,36,64]{3,2,1,0:T(8,128)(2,1)} %copy-done.10), kind=kOutput, calls=%fused_computation.11 | convolution fusion | flops 231798528 | bytes 14461440 | tf_op jit(solution)/shard_map/bthd,bchd->bthc/dot_general | solution.py:63
  46.4 3.3 %fusion.24 = f32[2,36,32,64]{3,2,1,0:T(8,128)} fusion(bf16[2,768,36,64]{1,3,2,0:T(8,128)(2,1)S(1)} %bitcast.128, f32[2,36,768,32]{2,3,1,0:T(8,128)S(1)} %get-tuple-element.15, f32[2,32,36]{1,2,0:T(8,128)S(1)} %max.36, pred[2,768]{1,0:T(4,128)(4,1)S(1)} %iota_compare_fusion.4), kind=kOutput, calls=%fused_computation.31 | convolution fusion | flops 233570304 | bytes 14756352 | tf_op jit(solution)/shard_map/bthc,bchd->bthd/dot_general | solution.py:79
  49.7 2.4 fusion.37
  52.5 0.3 fusion.63
  52.9 4.0 %fusion.10 = f32[2,32,36]{1,2,0:T(8,128)S(1)} fusion(f32[2,36,768,32]{2,3,1,0:T(8,128)} %copy-done.2, f32[2,32,36]{1,2,0:T(8,128)S(1)} %max.36, pred[2,768]{1,0:T(4,128)(4,1)S(1)} %iota_compare_fusion.4), kind=kLoop, calls=%fused_computation.20 | loop fusion | flops 7075584 | bytes 7097856 | tf_op jit(solution)/shard_map/reduce_sum | solution.py:78
  58.0 12.5 %copy.76 = bf16[2,512,2304]{1,2,0:T(8,128)(2,1)} copy(bf16[2,512,2304]{2,0,1:T(2,128)(2,1)} %all-gather.4.cloned.1.call-done) | data formatting | bytes 9437184 | tf_op jit(solution)/shard_map/all_gather | solution.py:99
  70.5 3.4 %fusion.2 = (f32[64,36]{0,1:T(8,128)S(1)}, f32[36,2,512,64]{2,3,1,0:T(8,128)S(1)}) fusion(pred[64,2]{0,1:T(4,128)(4,1)S(1)} %iota_compare_fusion.5, bf16[2,512,36,64]{1,3,2,0:T(8,128)(2,1)} %bitcast.125, bf16[64,36,64,1]{2,1,0,3:T(8,128)(2,1)S(1)} %bitcast.130), kind=kOutput, calls=%fused_computation.9 | convolution fusion | flops 309065472 | bytes 14460032 | tf_op jit(solution)/shard_map/rhd,gkhd->rhgk/dot_general | solution.py:105
  73.9 2.3 fusion
  76.2 1.6 copy-done.1
  77.8 0.4 bitcast_multiply_fusion
  78.1 14.3 %all-gather.6.cloned.1.call-done = bf16[2,512,2304]{2,0,1:T(2,128)(2,1)} async-done(((bf16[2,64,2304]{2,0,1:T(2,128)(2,1)}), bf16[2,512,2304]{2,0,1:T(2,128)(2,1)}) %all-gather.6.cloned.1.call-update) | async-done | bytes 4718608 | tf_op jit(solution)/shard_map/all_gather | solution.py:100
  92.4 12.4 %copy.80 = bf16[2,512,2304]{1,2,0:T(8,128)(2,1)} copy(bf16[2,512,2304]{2,0,1:T(2,128)(2,1)} %all-gather.6.cloned.1.call-done) | data formatting | bytes 9437184 | tf_op jit(solution)/shard_map/all_gather | solution.py:100
  104.8 7.3 %divide_convert_fusion = bf16[64,36,64]{2,0,1:T(8,128)(2,1)S(1)} fusion(f32[64,36,64]{2,0,1:T(8,128)S(1)} %bitcast_multiply_fusion, bf16[2,512,36,64]{1,3,2,0:T(8,128)(2,1)} %bitcast.129, f32[36,2,512,64]{2,3,1,0:T(8,128)} %copy-done.1, f32[64,36]{0,1:T(8,128)S(1)} %max.38, pred[64,2]{0,1:T(4,128)(4,1)S(1)} %iota_compare_fusion.5, ...), kind=kOutput, calls=%fused_computation.46 | convolution fusion | flops 311869440 | bytes 15059072 | tf_op jit(solution)/shard_map/rhgk,gkhd->rhd/dot_general | solution.py:113
  112.1 0.4 copy.83
  112.5 0.4 convert_element_type.75
  112.9 0.2 multiply_reduce_fusion.1
  113.4 0.3 broadcast_in_dim.88
  113.7 0.2 reshape.339
  113.9 1.6 scatter_custom_fusion
  115.5 0.2 reshape_reshape.7
  115.7 16.2 %all_to_all.10 = bf16[8,18,2304]{2,1,0:T(8,128)(2,1)S(1)} all-to-all(bf16[8,18,2304]{2,1,0:T(8,128)(2,1)S(1)} %reshape_reshape.7), channel_id=1, replica_groups=mesh['req'=4,'exp'=8] {'exp'}, dimensions={0} | all-to-all | bytes 1327104 | tf_op jit(solution)/shard_map/all_to_all | solution.py:149
  131.9 1.0 reshape.301
  133.0 54.6 %all-gather.8.cloned.1.call-done = bf16[576,2304]{1,0:T(8,128)(2,1)} async-done(((bf16[144,2304]{1,0:T(8,128)(2,1)}), bf16[576,2304]{1,0:T(8,128)(2,1)}) %all-gather.8.cloned.1.call-update) | async-done | bytes 2654224 | tf_op jit(solution)/shard_map/all_gather | solution.py:150
  187.6 9.7 %fusion.8 = f32[576,1440]{1,0:T(8,128)} fusion(bf16[576,2304]{1,0:T(8,128)(2,1)} %all-gather.8.cloned.1.call-done, bf16[1,2304,1440]{1,2,0:T(8,128)(2,1)} %param.33), kind=kOutput, calls=%fused_computation.18 | convolution fusion | flops 3822059520 | bytes 12607488 | tf_op jit(solution)/shard_map/dot_general | solution.py:151
  197.3 16.7 %fusion.21 = bf16[576,2304]{1,0:T(8,128)(2,1)} fusion(bf16[1,1440,2304]{2,1,0:T(8,128)(2,1)} %param.35, f32[576,1440]{1,0:T(8,128)} %fusion.8, bf16[576,2304]{1,0:T(8,128)(2,1)} %all-gather.8.cloned.1.call-done, bf16[1,2304,1440]{1,2,0:T(8,128)(2,1)} %param.34), kind=kOutput, calls=%fused_computation.30 | convolution fusion | flops 7650422784 | bytes 21897216 | tf_op jit(solution)/shard_map/dot_general | solution.py:155
  214.4 0.8 gather_fusion.2
  215.3 0.8 gather_fusion.3
  216.8 0.7 pad_maximum_fusion
  217.4 48.2 %reduce-scatter.2.cloned.1.call-done = bf16[144,2304]{1,0:T(8,128)(2,1)} async-done(((bf16[576,2304]{1,0:T(8,128)(2,1)}), bf16[144,2304]{1,0:T(8,128)(2,1)}) %reduce-scatter.2.cloned.1.call-update) | async-done | bytes 663568 | tf_op jit(solution)/shard_map/reduce_scatter | solution.py:154
  265.6 2.2 reshape.302
  267.8 3.8 %all-to-all-start.1 = ((bf16[8,18,2304]{2,1,0:T(8,128)(2,1)}), bf16[8,18,2304]{2,1,0:T(8,128)(2,1)S(1)}, u32[]{:S(2)}, u32[]{:S(2)}) async-start(bf16[8,18,2304]{2,1,0:T(8,128)(2,1)} %reshape.302), calls=%async_computation.2 | async-start | bytes 1769472 | tf_op jit(solution)/shard_map/all_to_all | solution.py:160
  271.7 1.1 gather_fusion.1
  273.2 11.9 %all-to-all-done.1 = bf16[8,18,2304]{2,1,0:T(8,128)(2,1)S(1)} async-done(((bf16[8,18,2304]{2,1,0:T(8,128)(2,1)}), bf16[8,18,2304]{2,1,0:T(8,128)(2,1)S(1)}, u32[]{:S(2)}, u32[]{:S(2)}) %all-to-all-start.1) | async-done | bytes 663584 | tf_op jit(solution)/shard_map/all_to_all | solution.py:160
  285.1 0.2 reshape.308
  285.3 1.1 gather_fusion
  286.4 0.7 reshape.322
  287.1 1.6 multiply_reduce_fusion
  288.8 0.8 add_convert_fusion
  (108 shorter events, 4.3 us)
Async XLA Ops:
  7.2 264.4 %copy-start = (bf16[2304,8]{0,1:T(8,128)(2,1)S(1)}, bf16[2304,8]{0,1:T(8,128)(2,1)}, u32[]{:S(2)}) copy-start(bf16[2304,8]{0,1:T(8,128)(2,1)} %param.32) | copy-start | bytes 110596
  7.2 50.8 %all-gather.4.cloned.1.call-start = ((), (), s32[]{:S(2)}) async-start(), calls=%async_computation.3 | async-start | bytes 5308416 | tf_op jit(solution)/shard_map/all_gather | solution.py:99
  9.8 82.6 %all-gather.6.cloned.1.call-start = ((), (), s32[]{:S(2)}) async-start(), calls=%async_computation.4 | async-start | bytes 5308416 | tf_op jit(solution)/shard_map/all_gather | solution.py:100
  12.3 175.2 %all-gather.8.cloned.1.call-start = ((), (), s32[]{:S(2)}) async-start(), calls=%async_computation.5 | async-start | bytes 3317760 | tf_op jit(solution)/shard_map/all_gather | solution.py:150
  13.8 26.2 %copy-start.10 = (bf16[2,32,36,64]{3,2,1,0:T(8,128)(2,1)}, bf16[2,32,36,64]{3,2,1,0:T(8,128)(2,1)S(1)}, u32[]{:S(2)}) copy-start(bf16[2,32,36,64]{3,2,1,0:T(8,128)(2,1)S(1)} %reshape.291) | copy-start | bytes 884740
  26.7 10.4 %copy-start.4 = (bf16[2,32,2304]{2,1,0:T(8,128)(2,1)S(1)}, bf16[2,32,2304]{2,1,0:T(8,128)(2,1)}, u32[]{:S(2)}) copy-start(bf16[2,32,2304]{2,1,0:T(8,128)(2,1)} %param.21) | copy-start | bytes 884740
  26.7 10.9 %copy-start.17 = (s32[2,32]{1,0:T(2,128)S(1)}, s32[2,32]{1,0:T(2,128)}, u32[]{:S(2)}) copy-start(s32[2,32]{1,0:T(2,128)} %param.23) | copy-start | bytes 772
  26.7 11.9 %copy-start.5 = (bf16[2,32,2304]{2,1,0:T(8,128)(2,1)S(1)}, bf16[2,32,2304]{2,1,0:T(8,128)(2,1)}, u32[]{:S(2)}) copy-start(bf16[2,32,2304]{2,1,0:T(8,128)(2,1)} %param.22) | copy-start | bytes 884740
  26.7 13.2 %copy-start.16 = (s32[2]{0:T(128)S(1)}, s32[2]{0:T(128)}, u32[]{:S(2)}) copy-start(s32[2]{0:T(128)} %param.26) | copy-start | bytes 28
  40.0 6.4 %slice-start = ((s8[7077888]{0:T(1024)(128)(4,1)}), s8[4194304]{0:T(1024)(128)(4,1)S(1)}, s32[]{:S(2)}) async-start(s8[7077888]{0:T(1024)(128)(4,1)} %bitcast.126), calls=%async_computation.7 | async-start | bytes 8388608
  41.4 5.0 %slice-start.1 = ((s8[7077888]{0:T(1024)(128)(4,1)}), s8[2883584]{0:T(1024)(128)(4,1)S(1)}, s32[]{:S(2)}) async-start(s8[7077888]{0:T(1024)(128)(4,1)} %bitcast.126), calls=%async_computation.8 | async-start | bytes 5767168
  46.3 3.4 %copy-start.2 = (f32[2,36,768,32]{2,3,1,0:T(8,128)}, f32[2,36,768,32]{2,3,1,0:T(8,128)S(1)}, u32[]{:S(2)}) copy-start(f32[2,36,768,32]{2,3,1,0:T(8,128)S(1)} %get-tuple-element.15) | copy-start | bytes 21233668
  49.7 2.6 copy-start.18
  49.7 2.8 copy-start.3
  52.3 4.7 %copy-start.13 = (s32[2,32,2]{1,2,0:T(2,128)S(1)}, s32[2,32,2]{1,2,0:T(2,128)}, u32[]{:S(2)}) copy-start(s32[2,32,2]{1,2,0:T(2,128)} %param.36) | copy-start | bytes 1540
  57.9 12.5 %copy-start.9 = (bf16[64,36,64]{2,1,0:T(8,128)(2,1)S(1)}, bf16[64,36,64]{2,1,0:T(8,128)(2,1)}, u32[]{:S(2)}) copy-start(bf16[64,36,64]{2,1,0:T(8,128)(2,1)} %reshape_reshape.6) | copy-start | bytes 884740
  73.8 3.9 %copy-start.1 = (f32[36,2,512,64]{2,3,1,0:T(8,128)}, f32[36,2,512,64]{2,3,1,0:T(8,128)S(1)}, u32[]{:S(2)}) copy-start(f32[36,2,512,64]{2,3,1,0:T(8,128)S(1)} %get-tuple-element.19) | copy-start | bytes 28311556
  104.8 8.1 %copy-start.11 = (bf16[2,32,2304]{2,1,0:T(8,128)(2,1)S(1)}, bf16[2,32,2304]{2,1,0:T(8,128)(2,1)}, u32[]{:S(2)}) copy-start(bf16[2,32,2304]{2,1,0:T(8,128)(2,1)} %param.30) | copy-start | bytes 884740
  104.8 8.5 %copy-start.14 = (f32[2304]{0:T(1024)S(1)}, f32[2304]{0:T(1024)}, u32[]{:S(2)}) copy-start(f32[2304]{0:T(1024)} %param.31) | copy-start | bytes 27652
  112.9 1.0 copy-start.7
  133.0 132.6 %reduce-scatter.2.cloned.1.call-start = ((), (), s32[]{:S(2)}) async-start(), calls=%async_computation.6 | async-start | bytes 3317760 | tf_op jit(solution)/shard_map/reduce_scatter | solution.py:154
  197.3 17.0 %copy-start.15 = (s32[2,8]{1,0:T(2,128)S(1)}, s32[2,8]{1,0:T(2,128)}, u32[]{:S(2)}) copy-start(s32[2,8]{1,0:T(2,128)} %param.37) | copy-start | bytes 196
  197.3 17.9 %copy-start.6 = (bf16[2,32,2304]{2,1,0:T(8,128)(2,1)S(1)}, bf16[2,32,2304]{2,1,0:T(8,128)(2,1)}, u32[]{:S(2)}) copy-start(bf16[2,32,2304]{2,1,0:T(8,128)(2,1)} %param.22) | copy-start | bytes 884740
  267.8 17.3 %all-to-all-start.1 = ((bf16[8,18,2304]{2,1,0:T(8,128)(2,1)}), bf16[8,18,2304]{2,1,0:T(8,128)(2,1)S(1)}, u32[]{:S(2)}, u32[]{:S(2)}) async-start(bf16[8,18,2304]{2,1,0:T(8,128)(2,1)} %reshape.302), calls=%async_computation.2 | async-start | bytes 1769472 | tf_op jit(solution)/shard_map/all_to_all | solution.py:160
  285.3 3.5 %copy-start.8 = (bf16[2,32,2304]{2,1,0:T(8,128)(2,1)S(1)}, bf16[2,32,2304]{2,1,0:T(8,128)(2,1)}, u32[]{:S(2)}) copy-start(bf16[2,32,2304]{2,1,0:T(8,128)(2,1)} %copy-done.7) | copy-start | bytes 884740
  285.3 3.5 %copy-start.12 = (bf16[2,32,2304]{2,1,0:T(8,128)(2,1)S(1)}, bf16[2,32,2304]{2,1,0:T(8,128)(2,1)}, u32[]{:S(2)}) copy-start(bf16[2,32,2304]{2,1,0:T(8,128)(2,1)} %param.30) | copy-start | bytes 884740
Sparse Core Ops, SparseCore 0:
  9.9 41.6 all-gather.3
  53.4 38.9 all-gather.5
  133.1 54.4 all-gather.7
  214.2 51.3 reduce-scatter.1
where the time goes:
time: 298 us; the launch traced here: 296 us
  waiting for transfers between devices  129 us (43%)
  local copies, waits for them, and re-layouts  71.3 us (24%)
  matrix products  50.2 us (17%)
  blocking collectives  16.2 us (5%)
  between operations  14.3 us (5%)
  other arithmetic  11.3 us (4%)
  starting transfers between devices  3.93 us (1%)
    all_gather x1, waiting for transfers between devices, on_device(): lax.all_gather(arrived.reshape(-1, width), 'req', axis=0, tiled=True)  54.6 us
    reduce_scatter x1, waiting for transfers between devices, on_device(): lax.psum_scatter(jnp.dot(hidden, down_local, preferred_element_type=jnp.f...  48.2 us
    unnamed x48, local copies, waits for them, and re-layouts  27.5 us
    dot_general x1, matrix products, on_device(): jnp.dot(hidden, down_local, preferred_element_type=jnp.float32)  16.7 us
    all_to_all x1, blocking collectives, on_device(): lax.all_to_all(outgoing, 'exp', split_axis=0, concat_axis=0, tiled=True)  16.2 us
    all_gather x1, waiting for transfers between devices, on_device(): value_piece = lax.all_gather(prompt_values, 'exp', axis=1, tiled=True)  14.3 us
    all_gather x1, local copies, waits for them, and re-layouts, on_device(): key_piece = lax.all_gather(prompt_keys, 'exp', axis=1, tiled=True)  12.5 us
    all_gather x1, local copies, waits for them, and re-layouts, on_device(): value_piece = lax.all_gather(prompt_values, 'exp', axis=1, tiled=True)  12.4 us
  transfers between devices with their start and end apart: 5, of which 4 were waited for; matrix products, arithmetic and copies ran while one was open for 24% of the time, Pallas kernels for 0%

commit v1 on v0

--- a/solution.py
+++ b/solution.py
@@ -96,8 +96,13 @@
     running_top = local_top
     summed = local_total
     gathered_acc = local_acc
-    key_piece = lax.all_gather(prompt_keys, "exp", axis=1, tiled=True)
-    value_piece = lax.all_gather(prompt_values, "exp", axis=1, tiled=True)
+    key_piece, value_piece = jnp.split(
+        lax.all_gather(
+            jnp.concatenate([prompt_keys, prompt_values], axis=0), "exp", axis=1, tiled=True
+        ),
+        [prompt_keys.shape[0]],
+        axis=0,
+    )
     key_count = key_piece.shape[1]
     key_heads = key_piece.reshape(GRP, key_count, HEADS, HDIM)
     value_heads = value_piece.reshape(GRP, key_count, HEADS, HDIM)

time: 298 us -> 306 us (1.027)
  local copies, waits for them, and re-layouts: 71.3 us -> 83.6 us
  matrix products: 50.2 us -> 45.6 us
    all_gather x2 -> x0, local copies, waits for them, and re-layouts: 24.9 us -> none  [the longest x1 12.5 us: on_device(): key_piece = lax.all_gather(prompt_keys, 'exp', axis=1, tiled=True)]
    unnamed x48 -> x40, local copies, waits for them, and re-layouts: 27.5 us -> 51.7 us
    split x0 -> x1, local copies, waits for them, and re-layouts: none -> 12.4 us  [on_device(): jnp.split(lax.all_gather(jnp.concatenate([prompt_keys, prompt_values], ax...]
    dot_general x1, matrix products: 7.34 us -> 1.38 us  [on_device(): jnp.einsum('rhgk,gkhd->rhd', block_weights.astype(jnp.bfloat16), value_he...]
    dot_general x1, matrix products: 3.3 us -> 7.17 us  [on_device(): jnp.einsum('bthc,bchd->bthd', cache_weights.astype(jnp.bfloat16), cache_v...]
    all_gather x2 -> x1, waiting for transfers between devices: 14.3 us -> 14.9 us  [on_device(): lax.all_gather(jnp.concatenate([prompt_keys, prompt_values], axis=0), 'ex...]
  transfers between devices with their start and end apart: 5 -> 4, of which waited for: 4 -> 4; matrix products, arithmetic and copies ran while one was open for 24% -> 16% of each run, Pallas kernels for 0% -> 0%
where the time goes in v1:
time: 306 us; the launch traced here: 304 us
  waiting for transfers between devices  130 us (42%)
  local copies, waits for them, and re-layouts  83.6 us (27%)
  matrix products  45.6 us (15%)
  blocking collectives  16.1 us (5%)
  between operations  14.3 us (5%)
  other arithmetic  11.3 us (4%)
  starting transfers between devices  3.93 us (1%)
    all_gather x1, waiting for transfers between devices, on_device(): lax.all_gather(arrived.reshape(-1, width), 'req', axis=0, tiled=True)  54.6 us
    unnamed x40, local copies, waits for them, and re-layouts  51.7 us
    reduce_scatter x1, waiting for transfers between devices, on_device(): lax.psum_scatter(jnp.dot(hidden, down_local, preferred_element_type=jnp.f...  48.2 us
    dot_general x1, matrix products, on_device(): jnp.dot(hidden, down_local, preferred_element_type=jnp.float32)  16.7 us
    all_to_all x1, blocking collectives, on_device(): lax.all_to_all(outgoing, 'exp', split_axis=0, concat_axis=0, tiled=True)  16.1 us
    all_gather x1, waiting for transfers between devices, on_device(): lax.all_gather(jnp.concatenate([prompt_keys, prompt_values], axis=0), 'ex...  14.9 us
    split x1, local copies, waits for them, and re-layouts, on_device(): jnp.split(lax.all_gather(jnp.concatenate([prompt_keys, prompt_values], ax...  12.4 us
    all_to_all x1, waiting for transfers between devices, on_device(): lax.all_to_all(summed_rows.reshape(holder_count, CAP, width), 'exp', spli...  11.9 us
  transfers between devices with their start and end apart: 4, of which 4 were waited for; matrix products, arithmetic and copies ran while one was open for 16% of the time, Pallas kernels for 0%

profile of v1, /device:TPU:0, one launch (start us, length us, event | category | flops | bytes accessed | tf_op | source)
XLA Modules:
  0.0 304.4 jit_solution(5355220500571321052)
XLA Ops:
  7.2 1.7 copy.78
  8.9 1.7 copy.79
  10.6 2.2 pad_maximum_fusion
  12.9 0.5 reshape.291
  13.4 0.5 reshape_reshape.6
  13.9 10.5 %copy.68 = bf16[2,768,2304]{1,2,0:T(8,128)(2,1)} copy(bf16[2,768,2304]{2,1,0:T(8,128)(2,1)} %param.24) | data formatting | bytes 14155776 | tf_op args[4]
  24.4 1.3 reshape.292
  25.7 0.2 fusion.50
  26.8 1.5 fusion.95
  28.3 4.4 %bitcast_reduce_fusion = (f32[2,32,36]{1,2,0:T(8,128)S(1)}, f32[2,36,768,32]{2,3,1,0:T(8,128)S(1)}) fusion(pred[2,768]{1,0:T(4,128)(4,1)S(1)} %iota_compare_fusion.4, bf16[2,768,36,64]{1,3,2,0:T(8,128)(2,1)} %bitcast.116, bf16[2,32,36,64]{3,2,1,0:T(8,128)(2,1)S(1)} %reshape.291), kind=kOutput, calls=%fused_computation.11 | convolution fusion | flops 231798528 | bytes 14461440 | tf_op jit(solution)/shard_map/bthd,bchd->bthc/dot_general | solution.py:63
  32.8 0.3 fusion.54
  33.1 2.5 copy-done.1
  35.6 1.7 fusion.10
  37.7 10.4 %copy.73 = bf16[2,768,2304]{1,2,0:T(8,128)(2,1)} copy(bf16[2,768,2304]{2,1,0:T(8,128)(2,1)} %param.25) | data formatting | bytes 14155776 | tf_op args[5]
  48.2 1.3 reshape.294
  49.5 7.2 %fusion.19 = f32[2,36,32,64]{3,2,1,0:T(8,128)S(1)} fusion(bf16[2,768,36,64]{1,3,2,0:T(8,128)(2,1)} %bitcast.118, f32[2,36,768,32]{2,3,1,0:T(8,128)} %copy-done.1, f32[2,32,36]{1,2,0:T(8,128)S(1)} %max.36, pred[2,768]{1,0:T(4,128)(4,1)S(1)} %iota_compare_fusion.4), kind=kOutput, calls=%fused_computation.27 | convolution fusion | flops 233570304 | bytes 14756352 | tf_op jit(solution)/shard_map/bthc,bchd->bthd/dot_general | solution.py:79
  56.7 0.4 fusion.30
  57.3 1.4 copy.83
  59.6 14.9 %all-gather.3.cloned.1.call-done = bf16[4,512,2304]{2,0,1:T(4,128)(2,1)} async-done(((bf16[4,64,2304]{2,0,1:T(4,128)(2,1)}), bf16[4,512,2304]{2,0,1:T(4,128)(2,1)}) %all-gather.3.cloned.1.call-update) | async-done | bytes 9437200 | tf_op jit(solution)/shard_map/all_gather | solution.py:100
  74.5 12.4 %fusion.94 = (bf16[2,512,2304]{2,0,1:T(2,128)(2,1)}, bf16[2,512,2304]{2,0,1:T(2,128)(2,1)}) fusion(bf16[4,512,2304]{2,0,1:T(4,128)(2,1)} %all-gather.3.cloned.1.call-done), kind=kLoop, calls=%fused_computation.134 | loop fusion | bytes 18874368 | tf_op jit(solution)/shard_map/split | solution.py:99
  86.9 12.3 %copy.101 = bf16[2,512,2304]{1,2,0:T(8,128)(2,1)} copy(bf16[2,512,2304]{2,0,1:T(2,128)(2,1)} %get-tuple-element.13) | data formatting | bytes 9437184
  99.2 12.4 %copy.102 = bf16[2,512,2304]{1,2,0:T(8,128)(2,1)} copy(bf16[2,512,2304]{2,0,1:T(2,128)(2,1)} %get-tuple-element.14) | data formatting | bytes 9437184
  111.6 3.4 %fusion.2 = (f32[64,36]{0,1:T(8,128)S(1)}, f32[36,2,512,64]{2,3,1,0:T(8,128)S(1)}) fusion(pred[64,2]{0,1:T(4,128)(4,1)S(1)} %iota_compare_fusion.5, bf16[2,512,36,64]{1,3,2,0:T(8,128)(2,1)} %bitcast.117, bf16[64,36,64,1]{2,1,0,3:T(8,128)(2,1)S(1)} %bitcast.121), kind=kOutput, calls=%fused_computation.9 | convolution fusion | flops 309065472 | bytes 14460032 | tf_op jit(solution)/shard_map/rhd,gkhd->rhgk/dot_general | solution.py:110
  115.0 2.7 fusion
  117.8 1.4 divide_convert_fusion
  119.2 0.4 copy.87
  119.6 0.4 convert_element_type.75
  120.0 0.2 multiply_reduce_fusion.1
  120.4 0.3 broadcast_in_dim.88
  120.7 1.0 reshape.339
  121.8 2.1 scatter_custom_fusion
  124.1 16.1 %all_to_all.10 = bf16[8,18,2304]{2,1,0:T(8,128)(2,1)S(1)} all-to-all(bf16[8,18,2304]{2,1,0:T(8,128)(2,1)S(1)} %reshape_reshape.7), channel_id=1, replica_groups=mesh['req'=4,'exp'=8] {'exp'}, dimensions={0} | all-to-all | bytes 1327104 | tf_op jit(solution)/shard_map/all_to_all | solution.py:154
  140.3 1.0 reshape.301
  141.4 54.6 %all-gather.5.cloned.1.call-done = bf16[576,2304]{1,0:T(8,128)(2,1)} async-done(((bf16[144,2304]{1,0:T(8,128)(2,1)}), bf16[576,2304]{1,0:T(8,128)(2,1)}) %all-gather.5.cloned.1.call-update) | async-done | bytes 2654224 | tf_op jit(solution)/shard_map/all_gather | solution.py:155
  195.9 9.7 %fusion.8 = f32[576,1440]{1,0:T(8,128)} fusion(bf16[576,2304]{1,0:T(8,128)(2,1)} %all-gather.5.cloned.1.call-done, bf16[1,2304,1440]{1,2,0:T(8,128)(2,1)} %param.33), kind=kOutput, calls=%fused_computation.18 | convolution fusion | flops 3822059520 | bytes 12607488 | tf_op jit(solution)/shard_map/dot_general | solution.py:156
  205.7 16.7 %fusion.16 = bf16[576,2304]{1,0:T(8,128)(2,1)} fusion(bf16[1,1440,2304]{2,1,0:T(8,128)(2,1)} %param.35, f32[576,1440]{1,0:T(8,128)} %fusion.8, bf16[576,2304]{1,0:T(8,128)(2,1)} %all-gather.5.cloned.1.call-done, bf16[1,2304,1440]{1,2,0:T(8,128)(2,1)} %param.34), kind=kOutput, calls=%fused_computation.26 | convolution fusion | flops 7650422784 | bytes 21897216 | tf_op jit(solution)/shard_map/dot_general | solution.py:160
  222.8 0.8 gather_fusion.2
  223.6 0.8 gather_fusion.3
  225.1 0.7 pad_maximum_fusion.1
  225.8 48.2 %reduce-scatter.2.cloned.1.call-done = bf16[144,2304]{1,0:T(8,128)(2,1)} async-done(((bf16[576,2304]{1,0:T(8,128)(2,1)}), bf16[144,2304]{1,0:T(8,128)(2,1)}) %reduce-scatter.2.cloned.1.call-update) | async-done | bytes 663568 | tf_op jit(solution)/shard_map/reduce_scatter | solution.py:159
  273.9 2.2 reshape.302
  276.1 3.8 %all-to-all-start.1 = ((bf16[8,18,2304]{2,1,0:T(8,128)(2,1)}), bf16[8,18,2304]{2,1,0:T(8,128)(2,1)S(1)}, u32[]{:S(2)}, u32[]{:S(2)}) async-start(bf16[8,18,2304]{2,1,0:T(8,128)(2,1)} %reshape.302), calls=%async_computation.2 | async-start | bytes 1769472 | tf_op jit(solution)/shard_map/all_to_all | solution.py:165
  280.1 1.1 gather_fusion.1
  281.6 11.9 %all-to-all-done.1 = bf16[8,18,2304]{2,1,0:T(8,128)(2,1)S(1)} async-done(((bf16[8,18,2304]{2,1,0:T(8,128)(2,1)}), bf16[8,18,2304]{2,1,0:T(8,128)(2,1)S(1)}, u32[]{:S(2)}, u32[]{:S(2)}) %all-to-all-start.1) | async-done | bytes 663584 | tf_op jit(solution)/shard_map/all_to_all | solution.py:165
  293.6 1.1 gather_fusion
  294.7 0.7 reshape.322
  295.4 1.6 multiply_reduce_fusion
  297.1 0.8 add_convert_fusion
  (96 shorter events, 4.6 us)
Async XLA Ops:
  7.2 272.8 %copy-start = (bf16[2304,8]{0,1:T(8,128)(2,1)S(1)}, bf16[2304,8]{0,1:T(8,128)(2,1)}, u32[]{:S(2)}) copy-start(bf16[2304,8]{0,1:T(8,128)(2,1)} %param.32) | copy-start | bytes 110596
  7.2 5.7 %copy-start.8 = (bf16[2,32,2304]{2,1,0:T(8,128)(2,1)S(1)}, bf16[2,32,2304]{2,1,0:T(8,128)(2,1)}, u32[]{:S(2)}) copy-start(bf16[2,32,2304]{2,1,0:T(8,128)(2,1)} %param.20) | copy-start | bytes 884740
  7.2 67.4 %all-gather.3.cloned.1.call-start = ((), (), s32[]{:S(2)}) async-start(), calls=%async_computation.3 | async-start | bytes 10616832 | tf_op jit(solution)/shard_map/all_gather | solution.py:100
  12.9 183.1 %all-gather.5.cloned.1.call-start = ((), (), s32[]{:S(2)}) async-start(), calls=%async_computation.4 | async-start | bytes 3317760 | tf_op jit(solution)/shard_map/all_gather | solution.py:155
  13.9 10.6 %copy-start.3 = (bf16[2,32,2304]{2,1,0:T(8,128)(2,1)S(1)}, bf16[2,32,2304]{2,1,0:T(8,128)(2,1)}, u32[]{:S(2)}) copy-start(bf16[2,32,2304]{2,1,0:T(8,128)(2,1)} %param.21) | copy-start | bytes 884740
  13.9 11.9 %copy-start.14 = (s32[2,32]{1,0:T(2,128)S(1)}, s32[2,32]{1,0:T(2,128)}, u32[]{:S(2)}) copy-start(s32[2,32]{1,0:T(2,128)} %param.23) | copy-start | bytes 772
  13.9 12.8 %copy-start.13 = (s32[2]{0:T(128)S(1)}, s32[2]{0:T(128)}, u32[]{:S(2)}) copy-start(s32[2]{0:T(128)} %param.26) | copy-start | bytes 28
  32.7 2.9 copy-start.1
  32.7 4.8 %copy-start.15 = (s32[2]{0:T(128)S(1)}, s32[2]{0:T(128)}, u32[]{:S(2)}) copy-start(s32[2]{0:T(128)} %param.29) | copy-start | bytes 28
  37.7 10.4 %copy-start.4 = (bf16[2,32,2304]{2,1,0:T(8,128)(2,1)S(1)}, bf16[2,32,2304]{2,1,0:T(8,128)(2,1)}, u32[]{:S(2)}) copy-start(bf16[2,32,2304]{2,1,0:T(8,128)(2,1)} %param.22) | copy-start | bytes 884740
  49.5 7.2 %copy-start.6 = (bf16[2,32,36,64]{3,2,1,0:T(8,128)(2,1)S(1)}, bf16[2,32,36,64]{3,2,1,0:T(8,128)(2,1)}, u32[]{:S(2)}) copy-start(bf16[2,32,36,64]{3,2,1,0:T(8,128)(2,1)} %reshape.294) | copy-start | bytes 884740
  56.7 2.0 copy-start.10
  115.0 2.7 copy-start.2
  115.0 2.7 copy-start.7
  117.8 2.2 copy-start.9
  117.8 2.5 copy-start.11
  120.0 177.1 %copy-start.5 = (bf16[2,32,2304]{2,1,0:T(8,128)(2,1)}, bf16[2,32,2304]{2,1,0:T(8,128)(2,1)S(1)}, u32[]{:S(2)}) copy-start(bf16[2,32,2304]{2,1,0:T(8,128)(2,1)S(1)} %convert_element_type.75) | copy-start | bytes 884740
  141.3 132.6 %reduce-scatter.2.cloned.1.call-start = ((), (), s32[]{:S(2)}) async-start(), calls=%async_computation.5 | async-start | bytes 3317760 | tf_op jit(solution)/shard_map/reduce_scatter | solution.py:159
  205.7 17.0 %copy-start.12 = (s32[2,8]{1,0:T(2,128)S(1)}, s32[2,8]{1,0:T(2,128)}, u32[]{:S(2)}) copy-start(s32[2,8]{1,0:T(2,128)} %param.37) | copy-start | bytes 196
  276.1 17.3 %all-to-all-start.1 = ((bf16[8,18,2304]{2,1,0:T(8,128)(2,1)}), bf16[8,18,2304]{2,1,0:T(8,128)(2,1)S(1)}, u32[]{:S(2)}, u32[]{:S(2)}) async-start(bf16[8,18,2304]{2,1,0:T(8,128)(2,1)} %reshape.302), calls=%async_computation.2 | async-start | bytes 1769472 | tf_op jit(solution)/shard_map/all_to_all | solution.py:165
Sparse Core Ops, SparseCore 0:
  13.0 61.5 all-gather.2
  141.5 54.4 all-gather.4
  222.5 51.3 reduce-scatter.1
